TPU v7x, 32 devices: a whole 2x2x4 slice. The times are simulated.
32 devices in a mesh: ctx: 8 (over z, x), tp: 4 (over y, core).
Axes of the slice: x: 2, y: 2, z: 4, core: 2. Of those that a mesh axis runs over, the one named last changes fastest.
Arguments:
- tokens: bfloat16 [4096, 4096], P(('ctx', 'tp')), may hold values from -6 to 6
- in_weight: bfloat16 [4096, 3, 4096], P('ctx', None, 'tp'), may hold values from -0.09375 to 0.09375
- short_filter: float32 [3, 3, 4096], P(None, None, 'tp'), may hold values from -3 to 3
- decay_rates: float32 [16, 4096], P(None, 'tp'), may hold values from 1.2207031e-05 to 0.1, as said below
- residues: float32 [16, 4096], P(None, 'tp'), may hold values from -1.5 to 1.5
- skip_gain: float32 [4096], P('tp'), may hold values from -4 to 4
Outputs:
- mixed: bfloat16 [4096, 4096], P('ctx', 'tp')
Inputs may be any that keep to these rules, and one draw needn't show every extreme that they name: `decay_rates`: positive decay rates.
All inputs are finite; a program needn't handle non-finite values.
Results may differ from a plain program's by a relative error of at most 0.0063.
Values may be sent and summed in bfloat16 or wider, within the bound.
A program may use at most 128 MiB of HBM per device.

v0:
```python
import jax
import jax.numpy as jnp
from jax import lax
from jax.sharding import PartitionSpec as P

BLOCK = 32


def passed_along(value, axis, steps):
    count = lax.axis_size(axis)
    initial, last = (max(0, -steps), min(count, count - steps))
    return lax.ppermute(value, axis, [(source, source + steps) for source in range(initial, last)])


def block_scan(product, decay_rates, residues, block):
    channels = product.shape[1]
    mode_gain = residues * jnp.sqrt(2.0 * decay_rates)
    positions = jnp.arange(block, dtype=jnp.float32)
    kernel = jnp.sum(
        mode_gain[None] * jnp.exp(-decay_rates[None] * positions[:, None, None]), axis=1
    )
    gaps = jnp.arange(block, dtype=jnp.int32)[:, None] - jnp.arange(block, dtype=jnp.int32)[None, :]
    toeplitz = jnp.where(
        (gaps >= 0)[:, :, None], kernel[jnp.clip(gaps, 0, block - 1)], jnp.float32(0.0)
    )
    read_out = mode_gain[None] * jnp.exp(-decay_rates[None] * (positions[:, None, None] + 1.0))
    take_in = jnp.exp(-decay_rates[None] * (block - 1.0 - positions)[:, None, None])
    step_decay = jnp.exp(-decay_rates * block)

    def advance(state, block_in):
        block_out = jnp.sum(toeplitz * block_in[None], axis=1) + jnp.sum(
            read_out * state[None], axis=1
        )
        state = step_decay * state + jnp.sum(take_in * block_in[:, None, :], axis=0)
        return (state, block_out)

    zero_state = jnp.zeros(decay_rates.shape, jnp.float32)
    state, outputs = lax.scan(advance, zero_state, product.reshape(-1, block, channels))
    return (outputs.reshape(-1, channels), state)


def per_device(tokens, in_weight, short_filter, decay_rates, residues, skip_gain):
    gathered = lax.all_gather(tokens, "tp", axis=0, tiled=True)
    length = gathered.shape[0]
    channels = in_weight.shape[2]
    short_lag = short_filter.shape[1] - 1
    flat_weight = in_weight.reshape(in_weight.shape[0], 3 * channels)
    projected = jnp.dot(
        gathered,
        lax.all_gather(flat_weight, "ctx", axis=0, tiled=True),
        preferred_element_type=jnp.float32,
    ).astype(jnp.bfloat16)
    prior_rows = passed_along(projected[length - short_lag :], "ctx", 1)
    padded = jnp.concatenate([prior_rows, projected], axis=0)
    widened = padded.astype(jnp.float32).reshape(length + short_lag, 3, channels)
    features = jnp.zeros((length, 3, channels), jnp.float32)
    for offset in range(short_lag + 1):
        features = (
            features
            + short_filter[None, :, offset, :]
            * widened[short_lag - offset : short_lag - offset + length]
        )
    product = features[:, 1] * features[:, 2]
    inside, outgoing = block_scan(product, decay_rates, residues, BLOCK)
    every_state = lax.all_gather(outgoing[None], "ctx", axis=0, tiled=True)
    shard_count = every_state.shape[0]
    own_index = lax.axis_index("ctx")
    sources = jnp.arange(shard_count, dtype=jnp.int32)
    distance = own_index - 1 - sources
    earlier = distance >= 0
    steps_back = jnp.where(earlier, distance, 0).astype(jnp.float32)
    factors = jnp.exp(-decay_rates[None] * (length * steps_back)[:, None, None])
    factors = jnp.where(earlier[:, None, None], factors, jnp.float32(0.0))
    incoming = jnp.sum(factors * every_state, axis=0)
    mode_gain = residues * jnp.sqrt(2.0 * decay_rates)
    offsets = jnp.arange(1, length + 1, dtype=jnp.float32)
    carried = jnp.sum(
        mode_gain[None] * jnp.exp(-decay_rates[None] * offsets[:, None, None]) * incoming[None],
        axis=1,
    )
    longconv = inside + carried
    return (features[:, 0] * (longconv + skip_gain[None] * product)).astype(jnp.bfloat16)


def solution(mesh):
    in_specs = (
        P(("ctx", "tp"), None),
        P("ctx", None, "tp"),
        P(None, None, "tp"),
        P(None, "tp"),
        P(None, "tp"),
        P("tp"),
    )
    out_specs = P("ctx", "tp")
    return jax.shard_map(
        per_device, mesh=mesh, in_specs=in_specs, out_specs=out_specs, check_vma=False
    )
```

profile of v0, /device:TPU:0, one launch (start us, length us, event | category | flops | bytes accessed | tf_op | source)
XLA Modules:
  0.0 757.3 jit_solution(17259507543595357559)
XLA Ops:
  7.3 4.6 copy.24
  12.7 5.4 gather_fusion
  18.2 4.9 broadcast_select_fusion.1
  23.2 22.9 %all-gather.4.cloned.1.call-done = bf16[512,4096]{1,0:T(8,128)(2,1)} async-done(((bf16[128,4096]{1,0:T(8,128)(2,1)}), bf16[512,4096]{1,0:T(8,128)(2,1)}) %all-gather.4.cloned.1.call-update) | async-done | bytes 4194320 | tf_op jit(solution)/shard_map/all_gather | solution.py:43
  46.1 481.9 %all-gather.6.cloned.1.call-done = bf16[4096,3072]{0,1:T(8,128)(2,1)} async-done(((bf16[512,3072]{0,1:T(8,128)(2,1)}), bf16[4096,3072]{0,1:T(8,128)(2,1)}) %all-gather.6.cloned.1.call-update) | async-done | bytes 25165840 | tf_op jit(solution)/shard_map/all_gather | solution.py:50
  528.0 18.2 %convolution_convert_fusion = bf16[512,3072]{1,0:T(8,128)(2,1)S(1)} fusion(bf16[512,4096]{1,0:T(8,128)(2,1)} %all-gather.4.cloned.1.call-done, bf16[4096,3072]{0,1:T(8,128)(2,1)} %all-gather.6.cloned.1.call-done), kind=kOutput, calls=%fused_computation.14 | convolution fusion | flops 12886474752 | bytes 32505856 | tf_op jit(solution)/shard_map/dot_general | solution.py:48
  552.8 6.6 fusion.10
  559.4 6.6 copy.29
  566.0 6.6 copy.30
  572.5 6.6 copy.27
  579.1 6.6 copy.28
  585.7 6.6 copy.25
  592.3 6.5 copy.26
  598.8 8.8 %multiply_add_fusion.1 = f32[512,3,1024]{2,0,1:T(8,128)S(1)} fusion(f32[512,3,1024]{2,0,1:T(8,128)} %copy.30, f32[512,3,1024]{2,0,1:T(8,128)} %copy.28, f32[512,3,1024]{2,0,1:T(8,128)} %copy.26, f32[3,1024]{1,0:T(4,128)S(1)} %get-tuple-element.187, f32[3,1024]{1,0:T(4,128)S(1)} %get-tuple-element.188, f32[3,1024]{1,0:T(4,128)S(1)} %bitcast.51), kind=kLoop, calls=%fused_computation.13 | loop fusion | flops 7864320 | bytes 25202688 | tf_op jit(solution)/shard_map/add | solution.py:59
  612.0 90.5 %while.15 = (s32[]{:T(128)}, f32[16,1024]{1,0:T(8,128)S(1)}, f32[16,32,1024]{2,1,0:T(8,128)}, f32[16,1024]{1,0:T(8,128)S(1)}, f32[16,32,1024]{2,1,0:T(8,128)}, /...) while((s32[]{:T(128)}, f32[16,1024]{1,0:T(8,128)S(1)}, ...), condition=%wide.region_5.6_spmd.clone.clone.clone, body=%wide.region_1.5_spmd.clone.clone.clone.sunk | while | flops 5783555 | bytes 6029712 | solution.py:38
  614.1 2.9 multiply_reduce_fusion.5
  619.8 2.9 multiply_reduce_fusion.5
  625.4 2.9 multiply_reduce_fusion.5
  631.1 2.9 multiply_reduce_fusion.5
  636.7 2.9 multiply_reduce_fusion.5
  642.4 2.9 multiply_reduce_fusion.5
  648.1 2.9 multiply_reduce_fusion.5
  653.7 2.9 multiply_reduce_fusion.5
  659.4 2.9 multiply_reduce_fusion.5
  670.7 2.9 multiply_reduce_fusion.5
  676.3 2.9 multiply_reduce_fusion.5
  682.0 2.9 multiply_reduce_fusion.5
  687.7 2.9 multiply_reduce_fusion.5
  693.3 2.9 multiply_reduce_fusion.5
  699.0 2.9 multiply_reduce_fusion.5
  702.6 34.3 %all-gather = f32[128,1024]{1,0:T(8,128)S(1)} all-gather(f32[16,1024]{1,0:T(8,128)S(1)} %get-tuple-element.49), channel_id=2, replica_groups=mesh['ctx'=8,'tp'=4] {'ctx'}, dimensions={0}, use_global_device_ids=true | all-gather | bytes 589824 | tf_op jit(solution)/shard_map/all_gather | solution.py:65
  737.1 11.0 %multiply_reduce_fusion.1 = f32[512,1024]{1,0:T(8,128)S(1)} fusion(f32[16,1024]{1,0:T(8,128)S(1)} %multiply_reduce_fusion.3, f32[512]{0:T(512)S(1)} %iota_add_fusion, f32[16,1024]{1,0:T(8,128)S(1)} %get-tuple-element.298, f32[16,1024]{1,0:T(8,128)S(1)} %get-tuple-element.299), kind=kLoop, calls=%fused_computation.12 | loop fusion | flops 33030144 | bytes 2295808 | tf_op jit(solution)/shard_map/reduce_sum | solution.py:77
  (126 shorter events, 61.6 us)
Async XLA Ops:
  6.5 39.6 %all-gather.4.cloned.1.call-start = ((), (), s32[]{:S(2)}) async-start(), calls=%async_computation | async-start | bytes 5242880 | tf_op jit(solution)/shard_map/all_gather | solution.py:43
  7.3 4.8 copy-start.3
  7.3 4.8 copy-start.4
  7.3 520.8 %all-gather.6.cloned.1.call-start = ((), (), s32[]{:S(2)}) async-start(), calls=%async_computation.1 | async-start | bytes 28311552 | tf_op jit(solution)/shard_map/all_gather | solution.py:50
  12.7 5.5 copy-start.5
  546.2 2.5 copy-start.1
  546.3 3.7 collective-permute-start
  607.6 2.7 copy-start
  736.9 11.3 %slice-start = ((s8[6291456]{0:T(1024)(128)(4,1)}), s8[4194304]{0:T(1024)(128)(4,1)S(1)}, s32[]{:S(2)}) async-start(s8[6291456]{0:T(1024)(128)(4,1)} %bitcast.42), calls=%async_computation.2 | async-start | bytes 8388608
  737.1 11.1 %slice-start.1 = ((s8[6291456]{0:T(1024)(128)(4,1)}), s8[2097152]{0:T(1024)(128)(4,1)S(1)}, s32[]{:S(2)}) async-start(s8[6291456]{0:T(1024)(128)(4,1)} %bitcast.42), calls=%async_computation.3 | async-start | bytes 4194304
  737.1 11.1 %copy-start.2 = (f32[16,32,1024]{2,1,0:T(8,128)S(1)}, f32[16,32,1024]{2,1,0:T(8,128)}, u32[]{:S(2)}) copy-start(f32[16,32,1024]{2,1,0:T(8,128)} %get-tuple-element.48) | copy-start | bytes 6291460
  737.1 11.1 %copy-start.6 = (f32[1024]{0:T(1024)S(1)}, f32[1024]{0:T(1024)}, u32[]{:S(2)}) copy-start(f32[1024]{0:T(1024)} %param.13) | copy-start | bytes 12292
Sparse Core Ops, SparseCore 0:
  8.9 37.1 all-gather.3
  47.6 480.3 all-gather.5
where the time goes:
time: 759 us; the launch traced here: 757 us
  waiting for transfers between devices  507 us (67%)
  other arithmetic  108 us (14%)
  local copies, waits for them, and re-layouts  73.6 us (10%)
  blocking collectives  34.3 us (5%)
  matrix products  18.2 us (2%)
  between operations  13.7 us (2%)
    all_gather x1, waiting for transfers between devices, per_device(): lax.all_gather(flat_weight, 'ctx', axis=0, tiled=True)  482 us
    reduce_sum x16, other arithmetic, advance(): jnp.sum(toeplitz * block_in[None], axis=1)  46.5 us
    slice x7, local copies, waits for them, and re-layouts, per_device(): widened[short_lag - offset:short_lag - offset + length]  46 us
    all_gather x1, blocking collectives, per_device(): every_state = lax.all_gather(outgoing[None], 'ctx', axis=0, tiled=True)  34.3 us
    all_gather x1, waiting for transfers between devices, per_device(): gathered = lax.all_gather(tokens, 'tp', axis=0, tiled=True)  22.9 us
    dot_general x1, matrix products, per_device(): jnp.dot(gathered, lax.all_gather(flat_weight, 'ctx', axis=0, tiled=True),...  18.2 us
    reduce_sum x16, other arithmetic, advance(): jnp.sum(read_out * state[None], axis=1)  17.7 us
  transfers between devices with their start and end apart: 3, of which 3 were waited for; matrix products, arithmetic and copies ran while one was open for 2% of the time, Pallas kernels for 0%

commit v1 on v0

--- a/solution.py
+++ b/solution.py
@@ -4,6 +4,16 @@
 from jax.sharding import PartitionSpec as P
 
 BLOCK = 32
+
+
+def gather_around(x, axis, dim):
+    ways, here, turn = (lax.axis_size(axis), lax.axis_index(axis), x.shape[dim])
+    lengths = [n * ways if d == dim else n for d, n in enumerate(x.shape)]
+    full = lax.dynamic_update_slice_in_dim(jnp.zeros(lengths, x.dtype), x, here * turn, axis=dim)
+    for far in range(1, ways):
+        x = lax.ppermute(x, axis, [(d, (d + 1) % ways) for d in range(ways)])
+        full = lax.dynamic_update_slice_in_dim(full, x, (here - far) % ways * turn, axis=dim)
+    return full
 
 
 def passed_along(value, axis, steps):
@@ -46,9 +56,7 @@
     short_lag = short_filter.shape[1] - 1
     flat_weight = in_weight.reshape(in_weight.shape[0], 3 * channels)
     projected = jnp.dot(
-        gathered,
-        lax.all_gather(flat_weight, "ctx", axis=0, tiled=True),
-        preferred_element_type=jnp.float32,
+        gathered, gather_around(flat_weight, "ctx", 0), preferred_element_type=jnp.float32
     ).astype(jnp.bfloat16)
     prior_rows = passed_along(projected[length - short_lag :], "ctx", 1)
     padded = jnp.concatenate([prior_rows, projected], axis=0)

time: 759 us -> 741 us (0.976)
  waiting for transfers between devices: 507 us -> 452 us
  local copies, waits for them, and re-layouts: 73.6 us -> 113 us
    all_gather x1 -> x0, waiting for transfers between devices: 482 us -> none  [per_device(): lax.all_gather(flat_weight, 'ctx', axis=0, tiled=True)]
    ppermute x0 -> x7, waiting for transfers between devices: none -> 451 us  [gather_around(): x = lax.ppermute(x, axis, [(d, (d + 1) % ways) for d in range(ways)])]
    all_gather x1, waiting for transfers between devices: 22.9 us -> 0.01 us  [per_device(): gathered = lax.all_gather(tokens, 'tp', axis=0, tiled=True)]
    dynamic_update_slice x0 -> x8, local copies, waits for them, and re-layouts: none -> 19.2 us  [the longest x7 17.3 us: gather_around(): lax.dynamic_update_slice_in_dim(full, x, (here - far) % ways * turn, axis...]
    unnamed x21 -> x39, local copies, waits for them, and re-layouts: 7.34 us -> 18.2 us
    broadcast_in_dim x0 -> x1, local copies, waits for them, and re-layouts: none -> 9.16 us  [gather_around(): jnp.zeros(lengths, x.dtype)]
  transfers between devices with their start and end apart: 3 -> 9, of which waited for: 3 -> 8; matrix products, arithmetic and copies ran while one was open for 2% -> 5% of each run, Pallas kernels for 0% -> 0%
where the time goes in v1:
time: 741 us; the launch traced here: 739 us
  waiting for transfers between devices  452 us (61%)
  local copies, waits for them, and re-layouts  113 us (15%)
  other arithmetic  106 us (14%)
  blocking collectives  31.3 us (4%)
  matrix products  18.2 us (2%)
  between operations  13.8 us (2%)
    ppermute x7, waiting for transfers between devices, gather_around(): x = lax.ppermute(x, axis, [(d, (d + 1) % ways) for d in range(ways)])  451 us
    reduce_sum x16, other arithmetic, advance(): jnp.sum(toeplitz * block_in[None], axis=1)  46.5 us
    slice x7, local copies, waits for them, and re-layouts, per_device(): widened[short_lag - offset:short_lag - offset + length]  46.1 us
    all_gather x1, blocking collectives, per_device(): every_state = lax.all_gather(outgoing[None], 'ctx', axis=0, tiled=True)  31.3 us
    dot_general x1, matrix products, per_device(): jnp.dot(gathered, gather_around(flat_weight, 'ctx', 0), preferred_element...  18.2 us
    unnamed x39, local copies, waits for them, and re-layouts  18.2 us
    reduce_sum x16, other arithmetic, advance(): jnp.sum(read_out * state[None], axis=1)  17.7 us
    dynamic_update_slice x7, local copies, waits for them, and re-layouts, gather_around(): lax.dynamic_update_slice_in_dim(full, x, (here - far) % ways * turn, axis...  17.3 us
  transfers between devices with their start and end apart: 9, of which 8 were waited for; matrix products, arithmetic and copies ran while one was open for 5% of the time, Pallas kernels for 0%

profile of v1, /device:TPU:0, one launch (start us, length us, event | category | flops | bytes accessed | tf_op | source)
XLA Modules:
  0.0 739.0 jit_solution(13917274328652521850)
XLA Ops:
  6.5 3.2 copy.24
  9.8 3.0 collective-permute-start
  12.8 71.1 %collective-permute-done = bf16[512,3072]{0,1:T(8,128)(2,1)S(1)} collective-permute-done((bf16[512,3072]{0,1:T(8,128)(2,1)S(1)}, bf16[512,3072]{0,1:T(8,128)(2,1)S(1)}, u32[]{:S(2)}, u32[]{:S(2)}) %collective-permute-start) | collective-permute-done | bytes 3145760 | tf_op jit(solution)/shard_map/ppermute | solution.py:14
  85.6 72.0 %collective-permute-done.1 = bf16[512,3072]{0,1:T(8,128)(2,1)S(1)} collective-permute-done((bf16[512,3072]{0,1:T(8,128)(2,1)S(1)}, bf16[512,3072]{0,1:T(8,128)(2,1)S(1)}, u32[]{:S(2)}, u32[]{:S(2)}) %collective-permute-start.1) | collective-permute-done | bytes 3145760 | tf_op jit(solution)/shard_map/ppermute | solution.py:14
  159.1 71.1 %collective-permute-done.2 = bf16[512,3072]{0,1:T(8,128)(2,1)S(1)} collective-permute-done((bf16[512,3072]{0,1:T(8,128)(2,1)S(1)}, bf16[512,3072]{0,1:T(8,128)(2,1)S(1)}, u32[]{:S(2)}, u32[]{:S(2)}) %collective-permute-start.2) | collective-permute-done | bytes 3145760 | tf_op jit(solution)/shard_map/ppermute | solution.py:14
  231.9 70.2 %collective-permute-done.3 = bf16[512,3072]{0,1:T(8,128)(2,1)S(1)} collective-permute-done((bf16[512,3072]{0,1:T(8,128)(2,1)S(1)}, bf16[512,3072]{0,1:T(8,128)(2,1)S(1)}, u32[]{:S(2)}, u32[]{:S(2)}) %collective-permute-start.3) | collective-permute-done | bytes 3145760 | tf_op jit(solution)/shard_map/ppermute | solution.py:14
  303.8 69.5 %collective-permute-done.4 = bf16[512,3072]{0,1:T(8,128)(2,1)} collective-permute-done((bf16[512,3072]{0,1:T(8,128)(2,1)S(1)}, bf16[512,3072]{0,1:T(8,128)(2,1)}, u32[]{:S(2)}, u32[]{:S(2)}) %collective-permute-start.4) | collective-permute-done | bytes 3145760 | tf_op jit(solution)/shard_map/ppermute | solution.py:14
  374.2 5.5 gather_fusion
  379.7 9.2 %broadcast_in_dim.35 = bf16[4096,3072]{0,1:T(8,128)(2,1)} broadcast(bf16[]{:T(256)} %constant.80.clone.1), dimensions={} | broadcast | bytes 25165826 | tf_op jit(solution)/shard_map/broadcast_in_dim | solution.py:12
  390.8 51.3 %collective-permute-done.5 = bf16[512,3072]{0,1:T(8,128)(2,1)} collective-permute-done((bf16[512,3072]{0,1:T(8,128)(2,1)}, bf16[512,3072]{0,1:T(8,128)(2,1)}, u32[]{:S(2)}, u32[]{:S(2)}) %collective-permute-start.5) | collective-permute-done | bytes 3145760 | tf_op jit(solution)/shard_map/ppermute | solution.py:14
  456.4 3.8 constant_dynamic-update-slice_fusion.2
  460.3 3.8 constant_dynamic-update-slice_fusion.1
  464.0 46.0 %collective-permute-done.6 = bf16[512,3072]{0,1:T(8,128)(2,1)S(1)} collective-permute-done((bf16[512,3072]{0,1:T(8,128)(2,1)}, bf16[512,3072]{0,1:T(8,128)(2,1)S(1)}, u32[]{:S(2)}, u32[]{:S(2)}) %collective-permute-start.6) | collective-permute-done | bytes 3145760 | tf_op jit(solution)/shard_map/ppermute | solution.py:14
  511.9 18.2 %fusion.6 = bf16[512,3072]{1,0:T(8,128)(2,1)S(1)} fusion(bf16[4096,3072]{0,1:T(8,128)(2,1)} %constant_dynamic-update-slice_fusion, bf16[512,4096]{1,0:T(8,128)(2,1)} %all-gather.3.cloned.1.call-done), kind=kOutput, calls=%fused_computation.15 | convolution fusion | flops 12886474752 | bytes 32505856 | tf_op jit(solution)/shard_map/dot_general | solution.py:58
  537.3 6.6 fusion.11
  543.9 6.6 copy.29
  550.5 6.6 copy.30
  557.1 6.6 copy.27
  563.7 6.6 copy.28
  570.3 6.6 copy.25
  576.8 6.5 copy.26
  583.4 8.8 %multiply_add_fusion.1 = f32[512,3,1024]{2,0,1:T(8,128)S(1)} fusion(f32[512,3,1024]{2,0,1:T(8,128)} %copy.30, f32[512,3,1024]{2,0,1:T(8,128)} %copy.28, f32[512,3,1024]{2,0,1:T(8,128)} %copy.26, f32[3,1024]{1,0:T(4,128)S(1)} %get-tuple-element.187, f32[3,1024]{1,0:T(4,128)S(1)} %get-tuple-element.188, f32[3,1024]{1,0:T(4,128)S(1)} %bitcast.54), kind=kLoop, calls=%fused_computation.13 | loop fusion | flops 7864320 | bytes 25202688 | tf_op jit(solution)/shard_map/add | solution.py:67
  596.6 90.7 %while.15 = (s32[]{:T(128)}, f32[16,1024]{1,0:T(8,128)S(1)}, f32[16,32,1024]{2,1,0:T(8,128)}, f32[16,1024]{1,0:T(8,128)S(1)}, f32[16,32,1024]{2,1,0:T(8,128)}, /...) while((s32[]{:T(128)}, f32[16,1024]{1,0:T(8,128)S(1)}, ...), condition=%wide.region_5.6_spmd.clone.clone.clone, body=%wide.region_1.5_spmd.clone.clone.clone.sunk | while | flops 5783555 | bytes 6029712 | solution.py:48
  604.4 2.9 multiply_reduce_fusion.5
  610.0 2.9 multiply_reduce_fusion.5
  615.7 2.9 multiply_reduce_fusion.5
  621.4 2.9 multiply_reduce_fusion.5
  627.0 2.9 multiply_reduce_fusion.5
  632.7 2.9 multiply_reduce_fusion.5
  644.0 2.9 multiply_reduce_fusion.5
  687.3 31.3 %all-gather = f32[128,1024]{1,0:T(8,128)S(1)} all-gather(f32[16,1024]{1,0:T(8,128)S(1)} %get-tuple-element.49), channel_id=2, replica_groups=mesh['ctx'=8,'tp'=4] {'ctx'}, dimensions={0}, use_global_device_ids=true | all-gather | bytes 589824 | tf_op jit(solution)/shard_map/all_gather | solution.py:73
  718.8 11.0 %multiply_reduce_fusion.1 = f32[512,1024]{1,0:T(8,128)S(1)} fusion(f32[16,1024]{1,0:T(8,128)S(1)} %multiply_reduce_fusion.3, f32[512]{0:T(512)S(1)} %iota_add_fusion, f32[16,1024]{1,0:T(8,128)S(1)} %get-tuple-element.305, f32[16,1024]{1,0:T(8,128)S(1)} %get-tuple-element.306), kind=kLoop, calls=%fused_computation.12 | loop fusion | flops 33030144 | bytes 2295808 | tf_op jit(solution)/shard_map/reduce_sum | solution.py:85
  (164 shorter events, 109.5 us)
Async XLA Ops:
  6.5 367.0 %copy-start.12 = (f32[16,1024]{1,0:T(8,128)S(1)}, f32[16,1024]{1,0:T(8,128)}, u32[]{:S(2)}) copy-start(f32[16,1024]{1,0:T(8,128)} %param.11) | copy-start | bytes 196612
  6.5 367.0 %copy-start.13 = (f32[16,1024]{1,0:T(8,128)S(1)}, f32[16,1024]{1,0:T(8,128)}, u32[]{:S(2)}) copy-start(f32[16,1024]{1,0:T(8,128)} %param.12) | copy-start | bytes 196612
  6.5 505.4 %all-gather.3.cloned.1.call-start = ((), (), s32[]{:S(2)}) async-start(), calls=%async_computation | async-start | bytes 5242880 | tf_op jit(solution)/shard_map/all_gather | solution.py:53
  9.8 74.2 %collective-permute-start = (bf16[512,3072]{0,1:T(8,128)(2,1)S(1)}, bf16[512,3072]{0,1:T(8,128)(2,1)S(1)}, u32[]{:S(2)}, u32[]{:S(2)}) collective-permute-start(bf16[512,3072]{0,1:T(8,128)(2,1)S(1)} %bitcast.50), channel_id=1, source_target_pairs={{0,4},{4,8},{8,12},{12,16},{16,20},{20,24},{24,28},{28,0},{1,5},{5... | collective-permute-start | bytes 9437192 | tf_op jit(solution)/shard_map/ppermute | solution.py:14
  83.9 1.6 copy-start.3
  85.6 72.0 %collective-permute-start.1 = (bf16[512,3072]{0,1:T(8,128)(2,1)S(1)}, bf16[512,3072]{0,1:T(8,128)(2,1)S(1)}, u32[]{:S(2)}, u32[]{:S(2)}) collective-permute-start(bf16[512,3072]{0,1:T(8,128)(2,1)S(1)} %collective-permute-done), channel_id=1, source_target_pairs={{0,4},{4,8},{8,12},{12,16},{16,20},{20,24},{24,28},{28,0},{1,5},{5... | collective-permute-start | bytes 9437192 | tf_op jit(solution)/shard_map/ppermute | solution.py:14
  157.5 1.6 copy-start.5
  159.1 71.1 %collective-permute-start.2 = (bf16[512,3072]{0,1:T(8,128)(2,1)S(1)}, bf16[512,3072]{0,1:T(8,128)(2,1)S(1)}, u32[]{:S(2)}, u32[]{:S(2)}) collective-permute-start(bf16[512,3072]{0,1:T(8,128)(2,1)S(1)} %collective-permute-done.1), channel_id=1, source_target_pairs={{0,4},{4,8},{8,12},{12,16},{16,20},{20,24},{24,28},{28,0},{1,5},{5... | collective-permute-start | bytes 9437192 | tf_op jit(solution)/shard_map/ppermute | solution.py:14
  230.2 1.6 copy-start.7
  231.9 70.3 %collective-permute-start.3 = (bf16[512,3072]{0,1:T(8,128)(2,1)S(1)}, bf16[512,3072]{0,1:T(8,128)(2,1)S(1)}, u32[]{:S(2)}, u32[]{:S(2)}) collective-permute-start(bf16[512,3072]{0,1:T(8,128)(2,1)S(1)} %collective-permute-done.2), channel_id=1, source_target_pairs={{0,4},{4,8},{8,12},{12,16},{16,20},{20,24},{24,28},{28,0},{1,5},{5... | collective-permute-start | bytes 9437192 | tf_op jit(solution)/shard_map/ppermute | solution.py:14
  302.1 1.7 copy-start.9
  303.8 69.5 %collective-permute-start.4 = (bf16[512,3072]{0,1:T(8,128)(2,1)S(1)}, bf16[512,3072]{0,1:T(8,128)(2,1)}, u32[]{:S(2)}, u32[]{:S(2)}) collective-permute-start(bf16[512,3072]{0,1:T(8,128)(2,1)S(1)} %collective-permute-done.3), channel_id=1, source_target_pairs={{0,4},{4,8},{8,12},{12,16},{16,20},{20,24},{24,28},{28,0},{1,5},{5... | collective-permute-start | bytes 9437192 | tf_op jit(solution)/shard_map/ppermute | solution.py:14
  373.3 68.9 %collective-permute-start.5 = (bf16[512,3072]{0,1:T(8,128)(2,1)}, bf16[512,3072]{0,1:T(8,128)(2,1)}, u32[]{:S(2)}, u32[]{:S(2)}) collective-permute-start(bf16[512,3072]{0,1:T(8,128)(2,1)} %collective-permute-done.4), channel_id=1, source_target_pairs={{0,4},{4,8},{8,12},{12,16},{16,20},{20,24},{24,28},{28,0},{1,5},{5... | collective-permute-start | bytes 9437192 | tf_op jit(solution)/shard_map/ppermute | solution.py:14
  374.2 5.5 copy-start.14
  388.9 53.3 %copy-start.1 = (f32[1024,1024]{1,0:T(8,128)S(1)}, f32[1024,1024]{1,0:T(8,128)}, u32[]{:S(2)}) copy-start(f32[1024,1024]{1,0:T(8,128)} %gather_fusion) | copy-start | bytes 12582916
  442.1 67.9 %collective-permute-start.6 = (bf16[512,3072]{0,1:T(8,128)(2,1)}, bf16[512,3072]{0,1:T(8,128)(2,1)S(1)}, u32[]{:S(2)}, u32[]{:S(2)}) collective-permute-start(bf16[512,3072]{0,1:T(8,128)(2,1)} %collective-permute-done.5), channel_id=1, source_target_pairs={{0,4},{4,8},{8,12},{12,16},{16,20},{20,24},{24,28},{28,0},{1,5},{5... | collective-permute-start | bytes 9437192 | tf_op jit(solution)/shard_map/ppermute | solution.py:14
  442.2 3.3 copy-start.4
  445.4 3.0 copy-start.6
  448.5 3.0 copy-start.8
  451.5 3.0 copy-start.10
  530.1 1.7 copy-start.2
  531.8 2.7 collective-permute-start.7
  592.2 2.7 copy-start
  718.6 11.2 %slice-start = ((s8[6291456]{0:T(1024)(128)(4,1)}), s8[4194304]{0:T(1024)(128)(4,1)S(1)}, s32[]{:S(2)}) async-start(s8[6291456]{0:T(1024)(128)(4,1)} %bitcast.44), calls=%async_computation.1 | async-start | bytes 8388608
  718.8 11.0 %slice-start.1 = ((s8[6291456]{0:T(1024)(128)(4,1)}), s8[2097152]{0:T(1024)(128)(4,1)S(1)}, s32[]{:S(2)}) async-start(s8[6291456]{0:T(1024)(128)(4,1)} %bitcast.44), calls=%async_computation.2 | async-start | bytes 4194304
  718.8 11.0 %copy-start.11 = (f32[16,32,1024]{2,1,0:T(8,128)S(1)}, f32[16,32,1024]{2,1,0:T(8,128)}, u32[]{:S(2)}) copy-start(f32[16,32,1024]{2,1,0:T(8,128)} %get-tuple-element.48) | copy-start | bytes 6291460
  718.8 11.0 %copy-start.15 = (f32[1024]{0:T(1024)S(1)}, f32[1024]{0:T(1024)}, u32[]{:S(2)}) copy-start(f32[1024]{0:T(1024)} %param.13) | copy-start | bytes 12292
Sparse Core Ops, SparseCore 0:
  373.4 35.1 all-gather.2
